TPU v7x, 32 devices: a whole 2x2x4 slice. The times are simulated.
32 devices in a mesh: groups: 2 (over y), chan: 4 (over z), tm: 2 (over core), dp: 2 (over x).
Axes of the slice: x: 2, y: 2, z: 4, core: 2. Of those that a mesh axis runs over, the one named last changes fastest.
Arguments:
- features: bfloat16 [384, 4, 8, 256], P('chan', ('groups', 'dp'), 'tm'), parts along dimension 1, may hold values from -6 to 6
- kernel: bfloat16 [384, 27, 384], P('chan'), may hold values from -0.078125 to 0.078125
- cotangent: bfloat16 [384, 4, 8, 256], P('chan', ('groups', 'dp'), 'tm'), parts along dimension 1, may hold values from -6 to 6
Outputs:
- conv_out: bfloat16 [384, 4, 8, 256], P('chan', ('groups', 'dp'), 'tm'), parts along dimension 1
- feature_grad: bfloat16 [384, 4, 8, 256], P('chan', ('groups', 'dp'), 'tm'), parts along dimension 1
- kernel_grad: float32 [768, 27, 384], P(('groups', 'chan')), parts along dimension 0
There are 2 independent parts, one for each index of `groups`. A program takes and returns all parts, laid end to end along the dimension named above; an argument that names none is the same for every part. Nothing has to cross between parts.
All inputs are finite; a program needn't handle non-finite values.
Results may differ from a plain program's by a relative error of at most 0.0051.
Values may be sent and summed in bfloat16 or wider, within the bound.
A program may use at most 128 MiB of HBM per device.

v0:
```python
import math
import jax
import jax.numpy as jnp
from jax import lax
from jax.sharding import PartitionSpec as P

WID = 64


def from_behind(x, axis, by):
    size = lax.axis_size(axis)
    pairs = [(i, i + by) for i in range(size) if 0 <= i + by < size]
    return lax.ppermute(x, axis, pairs)


def padded_copies(block):
    pixels = block.shape[-1]
    column = lax.broadcasted_iota(jnp.int32, (pixels,), 0) % WID
    nothing = jnp.zeros((), block.dtype)
    widths = [(0, 0), (0, 0), (0, 0), (WID + 1, WID + 1)]
    left_cut = jnp.pad(jnp.where(column == WID - 1, nothing, block), widths)
    untouched = jnp.pad(block, widths)
    right_cut = jnp.pad(jnp.where(column == 0, nothing, block), widths)
    return (left_cut, untouched, right_cut)


def tap_window(copies, first_frame, vertical, horizontal, frames, pixels):
    source = copies[horizontal]
    offset = vertical * WID + horizontal
    return source[:, :, first_frame : first_frame + frames, offset : offset + pixels]


def stacked_taps(copies, first_frame, flipped, frames, pixels):
    pieces = []
    for vertical in range(3):
        for horizontal in range(3):
            if flipped:
                pieces.append(
                    tap_window(copies, first_frame, 2 - vertical, 2 - horizontal, frames, pixels)
                )
            else:
                pieces.append(tap_window(copies, first_frame, vertical, horizontal, frames, pixels))
    concatenated = jnp.concatenate(pieces, axis=0)
    return concatenated.reshape(concatenated.shape[0], -1)


def local(features, kernel, cotangent):
    channels, clip_count, frames, pixels = features.shape
    flat_length = clip_count * frames * pixels
    widened = features.astype(jnp.float32)
    logistic = jax.nn.sigmoid(widened)
    activation = (widened * logistic).astype(jnp.bfloat16)
    slope_factor = logistic * (1.0 + widened * (1.0 - logistic))
    earlier = from_behind(activation[:, :, frames - 2 :, :], "tm", 1)
    extended = jnp.concatenate([earlier, activation], axis=2)
    upcoming = from_behind(cotangent[:, :, :2, :], "tm", -1)
    later_padded = jnp.concatenate([cotangent, upcoming], axis=2)
    cotangent_rows = cotangent.reshape(channels, -1)
    portion = lax.all_gather(extended, "chan", axis=0, tiled=True)
    out_sum = jnp.zeros((channels, flat_length), jnp.float32)
    amount = portion.shape[0]
    copies = padded_copies(portion)
    kernel_cols = kernel
    grad_parts = []
    for forward_temporal in range(3):
        stacked = stacked_taps(copies, forward_temporal, False, frames, pixels)
        weights = kernel_cols[:, 9 * forward_temporal : 9 * forward_temporal + 9, :].reshape(
            channels, 9 * amount
        )
        out_sum = out_sum + jnp.dot(weights, stacked, preferred_element_type=jnp.float32)
        grad_parts.append(
            lax.dot_general(
                cotangent_rows,
                stacked,
                (((1,), (1,)), ((), ())),
                preferred_element_type=jnp.float32,
            ).reshape(channels, 9, amount)
        )
    grad_sum = jnp.concatenate(grad_parts, axis=1)
    out_sum, grad_sum = (out_sum, grad_sum)
    conv_out = out_sum.reshape(features.shape).astype(jnp.bfloat16)
    position_count = lax.axis_size("dp") * lax.axis_size("tm") * flat_length
    kernel_grad = lax.psum(grad_sum, ("tm", "dp")) * (1.0 / math.sqrt(position_count))
    padded_later = padded_copies(later_padded)
    later_stacks = [
        stacked_taps(padded_later, 2 - temporal, True, frames, pixels) for temporal in range(3)
    ]
    amount = channels * lax.axis_size("chan")
    kernel_cols = kernel
    summed = jnp.zeros((amount, flat_length), jnp.float32)
    for temporal in range(3):
        weights = jnp.transpose(
            kernel_cols[:, 9 * temporal : 9 * temporal + 9, :], (2, 1, 0)
        ).reshape(amount, 9 * channels)
        summed = summed + jnp.dot(
            weights, later_stacks[temporal], preferred_element_type=jnp.float32
        )
    before_slope = lax.psum_scatter(
        summed.reshape(amount, clip_count, frames, pixels), "chan", scatter_dimension=0, tiled=True
    )
    feature_grad = (before_slope * slope_factor).astype(jnp.bfloat16)
    return (conv_out, feature_grad, kernel_grad)


def solution(mesh):
    return jax.shard_map(
        local,
        mesh=mesh,
        in_specs=(
            P("chan", ("groups", "dp"), "tm", None),
            P("chan", None, None),
            P("chan", ("groups", "dp"), "tm", None),
        ),
        out_specs=(
            P("chan", ("groups", "dp"), "tm", None),
            P("chan", ("groups", "dp"), "tm", None),
            P(("groups", "chan"), None, None),
        ),
        check_vma=False,
    )
```

profile of v0, /device:TPU:0, one launch (start us, length us, event | category | flops | bytes accessed | tf_op | source)
XLA Modules:
  0.0 263.4 jit_solution(15302708623575649266)
XLA Ops:
  8.2 1.4 collective-permute-start.1
  9.7 1.7 fusion.80
  23.0 1.6 copy.23
  24.7 38.9 %reduce-scatter.2.cloned.1.call-done = f32[96,1,4,256]{3,0,2,1:T(8,128)} async-done(((f32[384,1,4,256]{3,0,2,1:T(8,128)}), f32[96,1,4,256]{3,0,2,1:T(8,128)}) %reduce-scatter.2.cloned.1.call-update) | async-done | bytes 393232 | tf_op jit(solution)/shard_map/reduce_scatter | solution.py:98
  63.6 1.8 fusion.48
  65.4 1.4 collective-permute-start
  68.7 29.4 %all-gather.2.cloned.1.call-done = bf16[384,1,6,256]{3,0,2,1:T(8,128)(2,1)} async-done(((bf16[96,1,6,256]{3,0,2,1:T(8,128)(2,1)}), bf16[384,1,6,256]{3,0,2,1:T(8,128)(2,1)}) %all-gather.2.cloned.1.call-update) | async-done | bytes 1179664 | tf_op jit(solution)/shard_map/all_gather | solution.py:59
  98.1 1.5 broadcast_select_fusion
  102.1 1.7 fusion.31
  103.8 1.5 fusion.22
  105.3 1.7 fusion.40
  107.0 1.4 fusion.27
  108.5 1.6 slice_dynamic-update-slice_fusion.1
  111.3 1.5 fusion.28
  112.7 1.5 fusion.20
  114.2 1.4 fusion.37
  115.7 2.9 %copy-done.1 = bf16[3456,1,4,256]{3,0,2,1:T(8,128)(2,1)} copy-done((bf16[3456,1,4,256]{3,0,2,1:T(8,128)(2,1)}, bf16[3456,1,4,256]{3,0,2,1:T(8,128)(2,1)S(1)}, u32[]{:S(2)}) %copy-start.1) | copy-done | bytes 7077912
  118.6 2.2 fusion.6
  121.4 5.2 %fusion.9 = f32[96,3456]{1,0:T(8,128)S(1)} fusion(bf16[3456,1,4,256]{3,0,2,1:T(8,128)(2,1)} %get-tuple-element.27, bf16[96,4,256]{2,1,0:T(4,128)(2,1)S(1)} %bitcast.81), kind=kOutput, calls=%fused_computation.26 | convolution fusion | flops 679477248 | bytes 8601600 | tf_op jit(solution)/shard_map/dot_general | solution.py:72
  126.6 1.8 copy.27
  128.4 6.3 %fusion.12 = f32[96,3456]{1,0:T(8,128)} fusion(bf16[3456,1,4,256]{3,0,2,1:T(8,128)(2,1)} %copy-done.2, bf16[96,4,256]{2,1,0:T(4,128)(2,1)S(1)} %bitcast.82), kind=kOutput, calls=%fused_computation.27 | convolution fusion | flops 679477248 | bytes 8601600 | tf_op jit(solution)/shard_map/dot_general | solution.py:72
  134.7 3.4 %copy.29 = f32[96,3456]{0,1:T(8,128)} copy(f32[96,3456]{1,0:T(8,128)} %fusion.12) | data formatting | bytes 2654208 | tf_op jit(solution)/shard_map/dot_general | solution.py:72
  138.1 4.3 %pad_maximum_fusion = f32[96,27,384]{0,2,1:T(8,128)} fusion(f32[96,9,384]{0,2,1:T(8,128)} %bitcast.85, f32[96,9,384]{0,2,1:T(8,128)S(1)} %bitcast.84, f32[96,9,384]{0,2,1:T(8,128)S(1)} %bitcast.83), kind=kLoop, calls=%fused_computation.6 | loop fusion | flops 1990656 | bytes 7962624 | tf_op jit(solution)/shard_map/concatenate | solution.py:79
  146.4 9.9 %copy.17 = bf16[3456,1,4,256]{0,3,2,1:T(8,128)(2,1)} copy(bf16[3456,1,4,256]{3,0,2,1:T(8,128)(2,1)} %copy-done.1) | data formatting | bytes 14155776 | tf_op jit(solution)/shard_map/concatenate | solution.py:43
  156.2 10.3 %copy.19 = bf16[3456,1,4,256]{0,3,2,1:T(8,128)(2,1)} copy(bf16[3456,1,4,256]{3,0,2,1:T(8,128)(2,1)} %get-tuple-element.27) | data formatting | bytes 14155776 | tf_op jit(solution)/shard_map/concatenate | solution.py:43
  166.6 9.7 %copy.21 = bf16[3456,1,4,256]{0,3,2,1:T(8,128)(2,1)} copy(bf16[3456,1,4,256]{3,0,2,1:T(8,128)(2,1)} %copy-done.2) | data formatting | bytes 14155776 | tf_op jit(solution)/shard_map/concatenate | solution.py:43
  176.3 5.5 %fusion.81 = f32[1024,96]{0,1:T(8,128)S(1)} fusion(bf16[3456,1024]{0,1:T(8,128)(2,1)} %bitcast.77, bf16[96,3456]{0,1:T(8,128)(2,1)S(1)} %bitcast.89), kind=kOutput, calls=%fused_computation.148 | convolution fusion | flops 679477248 | bytes 8134656 | tf_op jit(solution)/shard_map/dot_general | solution.py:70
  181.8 2.3 convolution_add_fusion.1
  184.1 2.3 fusion.16
  187.2 58.2 %all-reduce.8.cloned.1.call-done = f32[96,27,384]{0,2,1:T(8,128)} async-done(((f32[96,27,384]{0,2,1:T(8,128)}), f32[96,27,384]{0,2,1:T(8,128)}) %all-reduce.8.cloned.1.call-update) | async-done | bytes 3981328 | tf_op jit(solution)/shard_map/psum | solution.py:83
  245.5 5.4 %broadcast_multiply_fusion = f32[96,27,384]{0,2,1:T(8,128)} fusion(f32[96,27,384]{0,2,1:T(8,128)} %all-reduce.8.cloned.1.call-done), kind=kLoop, calls=%fused_computation.34 | loop fusion | flops 995328 | bytes 7962624 | tf_op jit(solution)/shard_map/mul | solution.py:83
  250.9 6.0 %copy.32 = f32[96,27,384]{2,0,1:T(8,128)} copy(f32[96,27,384]{0,2,1:T(8,128)} %broadcast_multiply_fusion) | data formatting | bytes 7962624
  (82 shorter events, 23.3 us)
Async XLA Ops:
  7.2 56.4 %reduce-scatter.2.cloned.1.call-start = ((), (), s32[]{:S(2)}) async-start(), calls=%async_computation.2 | async-start | bytes 1966080 | tf_op jit(solution)/shard_map/reduce_scatter | solution.py:98
  8.2 3.3 %copy-start.4 = (bf16[96,1,4,256]{3,2,1,0:T(4,128)(2,1)S(1)}, bf16[96,1,4,256]{3,2,1,0:T(4,128)(2,1)}, u32[]{:S(2)}) copy-start(bf16[96,1,4,256]{3,2,1,0:T(4,128)(2,1)} %param.5) | copy-start | bytes 589828
  8.2 3.3 %collective-permute-start.1 = (bf16[96,1,2,256]{3,2,1,0:T(2,128)(2,1)S(1)}, bf16[96,1,2,256]{3,2,1,0:T(2,128)(2,1)S(1)}, u32[]{:S(2)}, u32[]{:S(2)}) collective-permute-start(bf16[96,1,2,256]{3,2,1,0:T(2,128)(2,1)S(1)} %slice.215), channel_id=1, source_target_pairs={{2,0},{3,1},{6,4},{7,5},{10,8},{11,9},{14,12},{15,13},{18,16},{19,... | collective-permute-start | bytes 294920 | tf_op jit(solution)/shard_map/ppermute | solution.py:13
  11.4 7.8 %copy-start.10 = (bf16[96,9,384]{2,0,1:T(8,128)(2,1)}, bf16[96,9,384]{2,0,1:T(8,128)(2,1)S(1)}, u32[]{:S(2)}) copy-start(bf16[96,9,384]{2,0,1:T(8,128)(2,1)S(1)} %get-tuple-element.10) | copy-start | bytes 1990660
  11.4 9.0 %copy-start.8 = (bf16[96,9,384]{2,0,1:T(8,128)(2,1)}, bf16[96,9,384]{2,0,1:T(8,128)(2,1)S(1)}, u32[]{:S(2)}) copy-start(bf16[96,9,384]{2,0,1:T(8,128)(2,1)S(1)} %get-tuple-element.11) | copy-start | bytes 1990660
  11.4 10.3 %copy-start.6 = (bf16[96,9,384]{2,0,1:T(8,128)(2,1)}, bf16[96,9,384]{2,0,1:T(8,128)(2,1)S(1)}, u32[]{:S(2)}) copy-start(bf16[96,9,384]{2,0,1:T(8,128)(2,1)S(1)} %get-tuple-element.9) | copy-start | bytes 1990660
  23.0 40.6 %copy-start.13 = (bf16[96,1,4,256]{3,2,1,0:T(4,128)(2,1)S(1)}, bf16[96,1,4,256]{3,2,1,0:T(4,128)(2,1)}, u32[]{:S(2)}) copy-start(bf16[96,1,4,256]{3,2,1,0:T(4,128)(2,1)} %param.3) | copy-start | bytes 589828
  24.6 73.5 %all-gather.2.cloned.1.call-start = ((), (), s32[]{:S(2)}) async-start(), calls=%async_computation.1 | async-start | bytes 1474560 | tf_op jit(solution)/shard_map/all_gather | solution.py:59
  65.4 2.3 collective-permute-start
  68.5 177.0 %all-reduce.8.cloned.1.call-start = ((), (), s32[]{:S(2)}) async-start(), calls=%async_computation.3 | async-start | bytes 10616832 | tf_op jit(solution)/shard_map/psum | solution.py:83
  98.1 1.8 copy-start
  107.0 8.6 %copy-start.2 = (bf16[3456,1,4,256]{3,0,2,1:T(8,128)(2,1)}, bf16[3456,1,4,256]{3,0,2,1:T(8,128)(2,1)S(1)}, u32[]{:S(2)}) copy-start(bf16[3456,1,4,256]{3,0,2,1:T(8,128)(2,1)S(1)} %get-tuple-element.12) | copy-start | bytes 21233668
  115.7 2.9 %copy-start.1 = (bf16[3456,1,4,256]{3,0,2,1:T(8,128)(2,1)}, bf16[3456,1,4,256]{3,0,2,1:T(8,128)(2,1)S(1)}, u32[]{:S(2)}) copy-start(bf16[3456,1,4,256]{3,0,2,1:T(8,128)(2,1)S(1)} %get-tuple-element.28) | copy-start | bytes 21233668
  134.7 3.4 %copy-start.5 = (f32[96,3456]{0,1:T(8,128)S(1)}, f32[96,3456]{0,1:T(8,128)}, u32[]{:S(2)}) copy-start(f32[96,3456]{0,1:T(8,128)} %copy.27) | copy-start | bytes 3981316
  142.4 1.1 copy-start.11
  143.5 1.1 copy-start.9
  143.5 1.5 copy-start.7
  143.5 2.0 copy-start.12
  176.3 5.5 %copy-start.3 = (bf16[3456,1,4,256]{0,3,2,1:T(8,128)(2,1)S(1)}, bf16[3456,1,4,256]{0,3,2,1:T(8,128)(2,1)}, u32[]{:S(2)}) copy-start(bf16[3456,1,4,256]{0,3,2,1:T(8,128)(2,1)} %copy.19) | copy-start | bytes 21233668
  176.3 7.8 %slice-start = ((s8[7077888]{0:T(1024)(128)(4,1)}), s8[4194304]{0:T(1024)(128)(4,1)S(1)}, s32[]{:S(2)}) async-start(s8[7077888]{0:T(1024)(128)(4,1)} %bitcast.73), calls=%async_computation.4 | async-start | bytes 8388608
  181.8 2.3 slice-start.1
Sparse Core Ops, SparseCore 0:
  24.7 38.8 reduce-scatter.1
  68.6 29.4 all-gather.1
  142.6 102.8 all-reduce.7
where the time goes:
time: 265 us; the launch traced here: 263 us
  waiting for transfers between devices  128 us (48%)
  local copies, waits for them, and re-layouts  76.3 us (29%)
  matrix products  27.6 us (10%)
  other arithmetic  14.7 us (6%)
  between operations  14.1 us (5%)
  starting transfers between devices  3.09 us (1%)
    psum x1, waiting for transfers between devices, local(): lax.psum(grad_sum, ('tm', 'dp')) * (1.0 / math.sqrt(position_count))  58.2 us
    reduce_scatter x1, waiting for transfers between devices, local(): lax.psum_scatter(summed.reshape(amount, clip_count, frames, pixels), 'cha...  38.9 us
    concatenate x7, local copies, waits for them, and re-layouts, stacked_taps(): concatenated = jnp.concatenate(pieces, axis=0)  34.2 us
    unnamed x64, local copies, waits for them, and re-layouts  29.9 us
    all_gather x1, waiting for transfers between devices, local(): portion = lax.all_gather(extended, 'chan', axis=0, tiled=True)  29.4 us
    dot_general x3, matrix products, local(): lax.dot_general(cotangent_rows, stacked, (((1,), (1,)), ((), ())), prefer...  13.8 us
    dot_general x3, matrix products, local(): jnp.dot(weights, stacked, preferred_element_type=jnp.float32)  10 us
    dot_general x3, local copies, waits for them, and re-layouts, local(): lax.dot_general(cotangent_rows, stacked, (((1,), (1,)), ((), ())), prefer...  5.72 us
  transfers between devices with their start and end apart: 5, of which 5 were waited for; matrix products, arithmetic and copies ran while one was open for 17% of the time, Pallas kernels for 0%

commit v1 on v0

--- a/solution.py
+++ b/solution.py
@@ -56,7 +56,12 @@
     upcoming = from_behind(cotangent[:, :, :2, :], "tm", -1)
     later_padded = jnp.concatenate([cotangent, upcoming], axis=2)
     cotangent_rows = cotangent.reshape(channels, -1)
-    portion = lax.all_gather(extended, "chan", axis=0, tiled=True)
+    ring = [extended]
+    for hop in range(3):
+        ring.append(lax.ppermute(ring[-1], "chan", [(dev, (dev + 1) % 4) for dev in range(4)]))
+    portion = jnp.roll(
+        jnp.concatenate(ring[::-1], axis=0), (lax.axis_index("chan") + 1) * ring[0].shape[0], axis=0
+    )
     out_sum = jnp.zeros((channels, flat_length), jnp.float32)
     amount = portion.shape[0]
     copies = padded_copies(portion)

time: 265 us -> 270 us (1.019)
  local copies, waits for them, and re-layouts: 76.3 us -> 83.3 us
    ppermute x0 -> x3, waiting for transfers between devices: none -> 30.5 us  [local(): lax.ppermute(ring[-1], 'chan', [(dev, (dev + 1) % 4) for dev in range(4)])]
    all_gather x1 -> x0, waiting for transfers between devices: 29.4 us -> none  [local(): portion = lax.all_gather(extended, 'chan', axis=0, tiled=True)]
    unnamed x64 -> x66, local copies, waits for them, and re-layouts: 29.9 us -> 35.6 us
  transfers between devices with their start and end apart: 5 -> 7, of which waited for: 5 -> 7; matrix products, arithmetic and copies ran while one was open for 17% -> 17% of each run, Pallas kernels for 0% -> 0%
where the time goes in v1:
time: 270 us; the launch traced here: 268 us
  waiting for transfers between devices  127 us (47%)
  local copies, waits for them, and re-layouts  83.3 us (31%)
  matrix products  27.6 us (10%)
  between operations  14.4 us (5%)
  other arithmetic  13 us (5%)
  starting transfers between devices  2.89 us (1%)
    psum x1, waiting for transfers between devices, local(): lax.psum(grad_sum, ('tm', 'dp')) * (1.0 / math.sqrt(position_count))  56.7 us
    reduce_scatter x1, waiting for transfers between devices, local(): lax.psum_scatter(summed.reshape(amount, clip_count, frames, pixels), 'cha...  38.9 us
    unnamed x66, local copies, waits for them, and re-layouts  35.6 us
    concatenate x7, local copies, waits for them, and re-layouts, stacked_taps(): concatenated = jnp.concatenate(pieces, axis=0)  35.4 us
    ppermute x3, waiting for transfers between devices, local(): lax.ppermute(ring[-1], 'chan', [(dev, (dev + 1) % 4) for dev in range(4)])  30.5 us
    dot_general x3, matrix products, local(): lax.dot_general(cotangent_rows, stacked, (((1,), (1,)), ((), ())), prefer...  13.8 us
    dot_general x3, matrix products, local(): jnp.dot(weights, stacked, preferred_element_type=jnp.float32)  10 us
    dot_general x3, local copies, waits for them, and re-layouts, local(): lax.dot_general(cotangent_rows, stacked, (((1,), (1,)), ((), ())), prefer...  5.78 us
  transfers between devices with their start and end apart: 7, of which 7 were waited for; matrix products, arithmetic and copies ran while one was open for 17% of the time, Pallas kernels for 0%

profile of v1, /device:TPU:0, one launch (start us, length us, event | category | flops | bytes accessed | tf_op | source)
XLA Modules:
  0.0 268.4 jit_solution(7460760572952312745)
XLA Ops:
  9.6 1.7 fusion.80
  22.9 1.6 copy.23
  24.6 38.9 %reduce-scatter.2.cloned.1.call-done = f32[96,1,4,256]{3,0,2,1:T(8,128)} async-done(((f32[384,1,4,256]{3,0,2,1:T(8,128)}), f32[96,1,4,256]{3,0,2,1:T(8,128)}) %reduce-scatter.2.cloned.1.call-update) | async-done | bytes 393232 | tf_op jit(solution)/shard_map/reduce_scatter | solution.py:103
  63.5 1.8 fusion.48
  67.8 11.0 %collective-permute-done.1 = bf16[96,1,6,256]{3,0,2,1:T(8,128)(2,1)S(1)} collective-permute-done((bf16[96,1,6,256]{3,0,2,1:T(8,128)(2,1)S(1)}, bf16[96,1,6,256]{3,0,2,1:T(8,128)(2,1)S(1)}, u32[]{:S(2)}, u32[]{:S(2)}) %collective-permute-start.1) | collective-permute-done | bytes 294944 | tf_op jit(solution)/shard_map/ppermute | solution.py:61
  78.8 10.2 %collective-permute-done.2 = bf16[96,1,6,256]{3,0,2,1:T(8,128)(2,1)S(1)} collective-permute-done((bf16[96,1,6,256]{3,0,2,1:T(8,128)(2,1)S(1)}, bf16[96,1,6,256]{3,0,2,1:T(8,128)(2,1)S(1)}, u32[]{:S(2)}, u32[]{:S(2)}) %collective-permute-start.2) | collective-permute-done | bytes 294944 | tf_op jit(solution)/shard_map/ppermute | solution.py:61
  89.0 9.4 %collective-permute-done.3 = bf16[96,1,6,256]{3,0,2,1:T(8,128)(2,1)S(1)} collective-permute-done((bf16[96,1,6,256]{3,0,2,1:T(8,128)(2,1)S(1)}, bf16[96,1,6,256]{3,0,2,1:T(8,128)(2,1)S(1)}, u32[]{:S(2)}, u32[]{:S(2)}) %collective-permute-start.3) | collective-permute-done | bytes 294944 | tf_op jit(solution)/shard_map/ppermute | solution.py:61
  99.1 1.4 fusion.29
  100.6 1.5 fusion.21
  102.1 1.5 fusion.38
  103.6 2.0 fusion.30
  109.2 2.2 dynamic-slice_dynamic-update-slice_fusion
  115.1 2.0 fusion.40
  117.1 1.5 fusion.28
  118.5 1.4 fusion.20
  120.0 1.5 fusion.37
  121.5 2.9 %copy-done = bf16[3456,1,4,256]{3,0,2,1:T(8,128)(2,1)} copy-done((bf16[3456,1,4,256]{3,0,2,1:T(8,128)(2,1)}, bf16[3456,1,4,256]{3,0,2,1:T(8,128)(2,1)S(1)}, u32[]{:S(2)}) %copy-start) | copy-done | bytes 7077912
  124.3 2.2 fusion.6
  127.1 5.2 %fusion.9 = f32[96,3456]{1,0:T(8,128)S(1)} fusion(bf16[3456,1,4,256]{3,0,2,1:T(8,128)(2,1)} %get-tuple-element.29, bf16[96,4,256]{2,1,0:T(4,128)(2,1)S(1)} %bitcast.81), kind=kOutput, calls=%fused_computation.26 | convolution fusion | flops 679477248 | bytes 8601600 | tf_op jit(solution)/shard_map/dot_general | solution.py:77
  132.3 2.0 copy.27
  134.4 6.3 %fusion.12 = f32[96,3456]{1,0:T(8,128)} fusion(bf16[3456,1,4,256]{3,0,2,1:T(8,128)(2,1)} %get-tuple-element.17, bf16[96,4,256]{2,1,0:T(4,128)(2,1)S(1)} %bitcast.82), kind=kOutput, calls=%fused_computation.27 | convolution fusion | flops 679477248 | bytes 8601600 | tf_op jit(solution)/shard_map/dot_general | solution.py:77
  140.7 3.2 %copy.29 = f32[96,3456]{0,1:T(8,128)} copy(f32[96,3456]{1,0:T(8,128)} %fusion.12) | data formatting | bytes 2654208 | tf_op jit(solution)/shard_map/dot_general | solution.py:77
  143.9 4.3 %pad_maximum_fusion = f32[96,27,384]{0,2,1:T(8,128)} fusion(f32[96,9,384]{0,2,1:T(8,128)} %bitcast.85, f32[96,9,384]{0,2,1:T(8,128)S(1)} %bitcast.84, f32[96,9,384]{0,2,1:T(8,128)S(1)} %bitcast.83), kind=kLoop, calls=%fused_computation.6 | loop fusion | flops 1990656 | bytes 7962624 | tf_op jit(solution)/shard_map/concatenate | solution.py:84
  151.7 10.5 %copy.17 = bf16[3456,1,4,256]{0,3,2,1:T(8,128)(2,1)} copy(bf16[3456,1,4,256]{3,0,2,1:T(8,128)(2,1)} %copy-done) | data formatting | bytes 14155776 | tf_op jit(solution)/shard_map/concatenate | solution.py:43
  162.2 10.4 %copy.19 = bf16[3456,1,4,256]{0,3,2,1:T(8,128)(2,1)} copy(bf16[3456,1,4,256]{3,0,2,1:T(8,128)(2,1)} %get-tuple-element.29) | data formatting | bytes 14155776 | tf_op jit(solution)/shard_map/concatenate | solution.py:43
  172.6 9.9 %copy.21 = bf16[3456,1,4,256]{0,3,2,1:T(8,128)(2,1)} copy(bf16[3456,1,4,256]{3,0,2,1:T(8,128)(2,1)} %get-tuple-element.17) | data formatting | bytes 14155776 | tf_op jit(solution)/shard_map/concatenate | solution.py:43
  182.6 5.5 %fusion.81 = f32[1024,96]{0,1:T(8,128)S(1)} fusion(bf16[3456,1024]{0,1:T(8,128)(2,1)} %bitcast.77, bf16[96,3456]{0,1:T(8,128)(2,1)S(1)} %bitcast.89), kind=kOutput, calls=%fused_computation.157 | convolution fusion | flops 679477248 | bytes 8134656 | tf_op jit(solution)/shard_map/dot_general | solution.py:75
  188.0 2.3 convolution_add_fusion.1
  190.4 2.3 fusion.16
  193.5 56.7 %all-reduce.8.cloned.1.call-done = f32[96,27,384]{0,2,1:T(8,128)} async-done(((f32[96,27,384]{0,2,1:T(8,128)}), f32[96,27,384]{0,2,1:T(8,128)}) %all-reduce.8.cloned.1.call-update) | async-done | bytes 3981328 | tf_op jit(solution)/shard_map/psum | solution.py:88
  250.1 5.4 %broadcast_multiply_fusion = f32[96,27,384]{0,2,1:T(8,128)} fusion(f32[96,27,384]{0,2,1:T(8,128)} %all-reduce.8.cloned.1.call-done), kind=kLoop, calls=%fused_computation.34 | loop fusion | flops 995328 | bytes 7962624 | tf_op jit(solution)/shard_map/mul | solution.py:88
  255.6 6.0 %copy.32 = f32[96,27,384]{2,0,1:T(8,128)} copy(f32[96,27,384]{0,2,1:T(8,128)} %broadcast_multiply_fusion) | data formatting | bytes 7962624
  (90 shorter events, 29.2 us)
Async XLA Ops:
  7.2 4.3 %copy-start.2 = (bf16[96,1,4,256]{3,2,1,0:T(4,128)(2,1)S(1)}, bf16[96,1,4,256]{3,2,1,0:T(4,128)(2,1)}, u32[]{:S(2)}) copy-start(bf16[96,1,4,256]{3,2,1,0:T(4,128)(2,1)} %param.5) | copy-start | bytes 589828
  7.2 56.3 %reduce-scatter.2.cloned.1.call-start = ((), (), s32[]{:S(2)}) async-start(), calls=%async_computation.1 | async-start | bytes 1966080 | tf_op jit(solution)/shard_map/reduce_scatter | solution.py:103
  8.3 3.2 %collective-permute-start.4 = (bf16[96,1,2,256]{3,2,1,0:T(2,128)(2,1)S(1)}, bf16[96,1,2,256]{3,2,1,0:T(2,128)(2,1)S(1)}, u32[]{:S(2)}, u32[]{:S(2)}) collective-permute-start(bf16[96,1,2,256]{3,2,1,0:T(2,128)(2,1)S(1)} %slice.215), channel_id=1, source_target_pairs={{2,0},{3,1},{6,4},{7,5},{10,8},{11,9},{14,12},{15,13},{18,16},{19,... | collective-permute-start | bytes 294920 | tf_op jit(solution)/shard_map/ppermute | solution.py:13
  11.3 7.8 %copy-start.8 = (bf16[96,9,384]{2,0,1:T(8,128)(2,1)}, bf16[96,9,384]{2,0,1:T(8,128)(2,1)S(1)}, u32[]{:S(2)}) copy-start(bf16[96,9,384]{2,0,1:T(8,128)(2,1)S(1)} %get-tuple-element.15) | copy-start | bytes 1990660
  11.3 9.0 %copy-start.6 = (bf16[96,9,384]{2,0,1:T(8,128)(2,1)}, bf16[96,9,384]{2,0,1:T(8,128)(2,1)S(1)}, u32[]{:S(2)}) copy-start(bf16[96,9,384]{2,0,1:T(8,128)(2,1)S(1)} %get-tuple-element.16) | copy-start | bytes 1990660
  11.3 10.3 %copy-start.4 = (bf16[96,9,384]{2,0,1:T(8,128)(2,1)}, bf16[96,9,384]{2,0,1:T(8,128)(2,1)S(1)}, u32[]{:S(2)}) copy-start(bf16[96,9,384]{2,0,1:T(8,128)(2,1)S(1)} %get-tuple-element.14) | copy-start | bytes 1990660
  22.9 40.6 %copy-start.11 = (bf16[96,1,4,256]{3,2,1,0:T(4,128)(2,1)S(1)}, bf16[96,1,4,256]{3,2,1,0:T(4,128)(2,1)}, u32[]{:S(2)}) copy-start(bf16[96,1,4,256]{3,2,1,0:T(4,128)(2,1)} %param.3) | copy-start | bytes 589828
  24.5 225.6 %all-reduce.8.cloned.1.call-start = ((), (), s32[]{:S(2)}) async-start(), calls=%async_computation.2 | async-start | bytes 10616832 | tf_op jit(solution)/shard_map/psum | solution.py:88
  65.3 2.3 collective-permute-start
  67.7 11.1 %collective-permute-start.1 = (bf16[96,1,6,256]{3,0,2,1:T(8,128)(2,1)S(1)}, bf16[96,1,6,256]{3,0,2,1:T(8,128)(2,1)S(1)}, u32[]{:S(2)}, u32[]{:S(2)}) collective-permute-start(bf16[96,1,6,256]{3,0,2,1:T(8,128)(2,1)S(1)} %pad_maximum_fusion.2), channel_id=1, source_target_pairs={{0,4},{4,8},{8,12},{12,0},{1,5},{5,9},{9,13},{13,1},{2,6},{6,10},{... | collective-permute-start | bytes 884744 | tf_op jit(solution)/shard_map/ppermute | solution.py:61
  78.8 10.2 %collective-permute-start.2 = (bf16[96,1,6,256]{3,0,2,1:T(8,128)(2,1)S(1)}, bf16[96,1,6,256]{3,0,2,1:T(8,128)(2,1)S(1)}, u32[]{:S(2)}, u32[]{:S(2)}) collective-permute-start(bf16[96,1,6,256]{3,0,2,1:T(8,128)(2,1)S(1)} %collective-permute-done.1), channel_id=1, source_target_pairs={{0,4},{4,8},{8,12},{12,0},{1,5},{5,9},{9,13},{13,1},{2,6},{6,10},{... | collective-permute-start | bytes 884744 | tf_op jit(solution)/shard_map/ppermute | solution.py:61
  89.0 9.4 %collective-permute-start.3 = (bf16[96,1,6,256]{3,0,2,1:T(8,128)(2,1)S(1)}, bf16[96,1,6,256]{3,0,2,1:T(8,128)(2,1)S(1)}, u32[]{:S(2)}, u32[]{:S(2)}) collective-permute-start(bf16[96,1,6,256]{3,0,2,1:T(8,128)(2,1)S(1)} %collective-permute-done.2), channel_id=1, source_target_pairs={{0,4},{4,8},{8,12},{12,0},{1,5},{5,9},{9,13},{13,1},{2,6},{6,10},{... | collective-permute-start | bytes 884744 | tf_op jit(solution)/shard_map/ppermute | solution.py:61
  121.4 2.9 %copy-start = (bf16[3456,1,4,256]{3,0,2,1:T(8,128)(2,1)}, bf16[3456,1,4,256]{3,0,2,1:T(8,128)(2,1)S(1)}, u32[]{:S(2)}) copy-start(bf16[3456,1,4,256]{3,0,2,1:T(8,128)(2,1)S(1)} %get-tuple-element.30) | copy-start | bytes 21233668
  140.7 3.2 %copy-start.3 = (f32[96,3456]{0,1:T(8,128)S(1)}, f32[96,3456]{0,1:T(8,128)}, u32[]{:S(2)}) copy-start(f32[96,3456]{0,1:T(8,128)} %copy.27) | copy-start | bytes 3981316
  148.2 1.1 copy-start.9
  148.2 1.5 copy-start.7
  149.3 1.1 copy-start.5
  149.3 1.6 copy-start.10
  182.6 5.5 %copy-start.1 = (bf16[3456,1,4,256]{0,3,2,1:T(8,128)(2,1)S(1)}, bf16[3456,1,4,256]{0,3,2,1:T(8,128)(2,1)}, u32[]{:S(2)}) copy-start(bf16[3456,1,4,256]{0,3,2,1:T(8,128)(2,1)} %copy.19) | copy-start | bytes 21233668
  182.6 7.8 %slice-start = ((s8[7077888]{0:T(1024)(128)(4,1)}), s8[4194304]{0:T(1024)(128)(4,1)S(1)}, s32[]{:S(2)}) async-start(s8[7077888]{0:T(1024)(128)(4,1)} %bitcast.73), calls=%async_computation.3 | async-start | bytes 8388608
  188.0 2.3 slice-start.1
Sparse Core Ops, SparseCore 0:
  24.6 38.8 reduce-scatter.1
  148.4 101.7 all-reduce.7
